TPU v7x, 32 devices: a whole 2x2x4 slice. The times are simulated.
32 devices in a mesh: dp: 8 (over y, x, core), seq: 4 (over z).
Axes of the slice: x: 2, y: 2, z: 4, core: 2. Of those that a mesh axis runs over, the one named last changes fastest.
Arguments:
- tokens: bfloat16 [8, 2048, 768], P('dp', 'seq'), may hold values from -6 to 6
- cotangent: bfloat16 [8, 2048, 768], P('dp', 'seq'), may hold values from -6 to 6
- segment_ids: int32 [8, 2048], P('dp', 'seq'), may hold values from 0 to 7, as said below
- doc_starts: int32 [8, 2048], P('dp', 'seq'), may hold values from 0 to 1, as said below
- valid_mask: int32 [8, 2048], P('dp', 'seq'), may hold values from 0 to 1
- step_number: int32 [1], replicated, may hold values from 1 to 64
- learn_rate: float32 [1], replicated, may hold values from 0.001 to 0.004
- norm_gain: float32 [768], replicated, may hold values from 0.5 to 1.5
- in_weight: bfloat16 [768, 3352], replicated, may hold values from -0.21875 to 0.21875
- conv_weight: float32 [4, 1792], replicated, may hold values from -3 to 3
- conv_bias: float32 [1792], replicated, may hold values from -1.75 to 1.75
- dt_bias: float32 [24], replicated, may hold values from -6 to -2
- a_log: float32 [24], replicated, may hold values from -1 to 2.5
- skip_d: float32 [24], replicated, may hold values from 0.5 to 1.5
- gate_gain: float32 [1536], replicated, may hold values from 0.5 to 1.5
- out_weight: bfloat16 [1536, 768], replicated, may hold values from -0.15625 to 0.15625
- in_momentum: float32 [768, 3352], P('seq'), may hold values from -6 to 6
- out_momentum: float32 [1536, 768], P(None, 'seq'), may hold values from -448 to 448
Outputs:
- output: bfloat16 [8, 2048, 768], P('dp', 'seq')
- input_grad: bfloat16 [8, 2048, 768], P('dp', 'seq')
- new_in_weight: bfloat16 [768, 3352], replicated
- new_out_weight: bfloat16 [1536, 768], replicated
- new_in_momentum: float32 [768, 3352], P('seq')
- new_out_momentum: float32 [1536, 768], P(None, 'seq')
- norm_gain_grad: float32 [768], replicated
- conv_weight_grad: float32 [4, 1792], replicated
- conv_bias_grad: float32 [1792], replicated
- dt_bias_grad: float32 [24], replicated
- a_log_grad: float32 [24], replicated
- skip_grad: float32 [24], replicated
- gate_gain_grad: float32 [1536], replicated
- output_rms: float32 [1], replicated
- mixer_rms: float32 [1], replicated
Inputs may be any that keep to these rules, and one draw needn't show every extreme that they name: Within each sequence segment_ids never fall, are 0 at the first position and rise by one exactly where doc_starts is 1; every sequence holds exactly 8 documents. `doc_starts`: 1 at the first position of every sequence; exactly 8 ones in every sequence.
All inputs are finite; a program needn't handle non-finite values.
Results may differ from a plain program's by a relative error of at most 0.0066.
The roundings to bfloat16 on the way count: a program that leaves them out, or rounds other values in their place, can miss the bound.
Values may be sent and summed in bfloat16 or wider, within the bound.
A program may use at most 192 MiB of HBM per device.

v0:
```python
import jax
import jax.numpy as jnp
from jax import lax
from jax.sharding import PartitionSpec as P

epsilon = 1e-05
highest = lax.Precision.HIGHEST


def shifted(block, axis, distance):
    devices = range(lax.axis_size(axis))
    route = [(i - distance, i) for i in devices if i - distance in devices]
    return lax.ppermute(block, axis, route)


def entering(value, axis, join, neutral):
    place = lax.axis_index(axis)
    gathered = jax.tree.map(
        lambda a, kind: lax.all_gather(a.astype(kind), axis), value, (jnp.bfloat16, jnp.bfloat16)
    )
    state = jax.tree.map(lambda a, e: jnp.zeros_like(a) + jnp.asarray(e, a.dtype), value, neutral)

    def one(step, state):
        return join(
            state,
            jax.tree.map(
                lambda a, own: lax.dynamic_index_in_dim(a, step, 0, False).astype(own.dtype),
                gathered,
                value,
            ),
        )

    return lax.fori_loop(0, place, one, state)


def carried_in(value, axis, combine, identity):
    length, mine = (lax.axis_size(axis), lax.axis_index(axis))
    everything = jax.tree.map(lambda part: lax.all_gather(part, axis), value)
    start = jax.tree.map(
        lambda part, zero: jnp.broadcast_to(jnp.asarray(zero, part.dtype), part.shape),
        value,
        identity,
    )

    def step(k, before):
        at = length - 1 - k
        reached = at > mine
        new = combine(before, jax.tree.map(lambda part: part[at], everything))
        return jax.tree.map(lambda a, b: jnp.where(reached, a, b), new, before)

    return lax.fori_loop(0, length, step, start)


def pre_norm(values, gain_values):
    return (
        values
        * lax.rsqrt(jnp.mean(values * values, axis=-1, keepdims=True) + epsilon)
        * gain_values
    )


def compose(earlier, later):
    return (earlier[0] * later[0], later[0][:, :, None, None] * earlier[1] + later[1])


def local(
    tokens,
    cotangent,
    segment_ids,
    doc_starts,
    valid_mask,
    step_number,
    learn_rate,
    norm_gain,
    in_weight,
    conv_weight,
    conv_bias,
    dt_bias,
    a_log,
    skip_d,
    gate_gain,
    out_weight,
    in_momentum,
    out_momentum,
):
    seq_count, piece_size, model_width = tokens.shape
    head_count = dt_bias.shape[0]
    tap_count, channels = conv_weight.shape
    inner_width = gate_gain.shape[0]
    state_width = (channels - inner_width) // 2
    head_width = inner_width // head_count
    proj_width = in_weight.shape[1]
    row_count = seq_count * piece_size
    inputs = tokens.astype(jnp.float32)
    normed_in, back_pre = jax.vjp(pre_norm, inputs, norm_gain)
    normed_low = normed_in.astype(jnp.bfloat16).reshape(row_count, model_width)
    projected = jnp.dot(normed_low, in_weight, preferred_element_type=jnp.float32).reshape(
        seq_count, piece_size, proj_width
    )
    gate_in = projected[:, :, :inner_width]
    conv_in = projected[:, :, inner_width : inner_width + channels]
    dt_raw = projected[:, :, inner_width + channels :]
    seg_float = segment_ids.astype(jnp.float32)
    prev_rows, prev_seg = shifted(
        (conv_in[:, piece_size - tap_count + 1 :], seg_float[:, piece_size - tap_count + 1 :]),
        "seq",
        1,
    )
    padded = jnp.concatenate([prev_rows, conv_in], axis=1)
    seg_pad = jnp.concatenate([prev_seg, seg_float], axis=1)
    masks = [
        (seg_pad[:, k : k + piece_size] == seg_float).astype(jnp.float32)[:, :, None]
        for k in range(tap_count)
    ]

    def conv_part(padded_in, taps_in, bias_in, raw_in, dt_bias_in, a_log_in):
        summed = bias_in + jnp.zeros((seq_count, piece_size, channels), jnp.float32)
        for k in range(tap_count):
            summed = summed + padded_in[:, k : k + piece_size] * masks[k] * taps_in[k]
        activated = jax.nn.silu(summed)
        signal = activated[:, :, :inner_width].reshape(
            seq_count, piece_size, head_count, head_width
        )
        writer = activated[:, :, inner_width : inner_width + state_width]
        reader = activated[:, :, inner_width + state_width :]
        step_size = jax.nn.softplus(raw_in + dt_bias_in)
        return (signal, writer, reader, step_size, -jnp.exp(a_log_in) * step_size)

    (signal, writer, reader, step_size, log_decay), back_conv = jax.vjp(
        conv_part, padded, conv_weight, conv_bias, dt_raw, dt_bias, a_log
    )
    counter = jnp.cumsum(doc_starts, axis=1)
    positions = jnp.arange(piece_size)
    causal = positions[:, None] >= positions[None, :]
    same_doc = (counter[:, :, None] == counter[:, None, :]) & causal[None]
    first_doc = (counter == 0)[:, :, None]
    last_doc = (counter == counter[:, -1:])[:, :, None]
    untouched = (counter[:, -1] == 0)[:, None]

    def end_state(signal_in, writer_in, step_in, decay_in):
        cumulative = jnp.cumsum(decay_in, axis=1)
        final_log = cumulative[:, -1]
        keeping = jnp.where(untouched, jnp.exp(final_log), 0.0)
        tails = jnp.where(last_doc, jnp.exp(final_log[:, None] - cumulative), 0.0) * step_in
        fresh_state = jnp.einsum(
            "slh,slhp,sln->shpn", tails, signal_in, writer_in, precision=highest
        )
        return (keeping, fresh_state)

    def piece_out(signal_in, writer_in, reader_in, step_in, decay_in, incoming_in):
        cumulative = jnp.cumsum(decay_in, axis=1)
        by_head = jnp.transpose(cumulative, (0, 2, 1))
        gaps = by_head[:, :, :, None] - by_head[:, :, None, :]
        decays = jnp.exp(jnp.where(same_doc[:, None], gaps, -1e30))
        scores = jnp.einsum("stn,sun->stu", reader_in, writer_in, precision=highest)
        weighted = scores[:, None] * decays
        inner_part = jnp.einsum(
            "shtu,suhp->sthp", weighted, signal_in * step_in[..., None], precision=highest
        )
        entries = jnp.where(first_doc, jnp.exp(cumulative), 0.0)
        carried = (
            jnp.einsum("stn,shpn->sthp", reader_in, incoming_in, precision=highest)
            * entries[..., None]
        )
        return inner_part + carried

    (keeping, fresh_state), back_end = jax.vjp(end_state, signal, writer, step_size, log_decay)
    identity = (jnp.ones_like(keeping), jnp.zeros_like(fresh_state))
    _, incoming = entering((keeping, fresh_state), "seq", compose, identity)
    ssm_out, back_out = jax.vjp(piece_out, signal, writer, reader, step_size, log_decay, incoming)

    def gate_norm(ssm_in, signal_in, skip_in, gate_values, gain_values):
        mixer_in = (ssm_in + skip_in[:, None] * signal_in).reshape(
            seq_count, piece_size, inner_width
        )
        gated_out = mixer_in * jax.nn.silu(gate_values)
        return (
            gated_out
            * lax.rsqrt(jnp.mean(gated_out * gated_out, axis=-1, keepdims=True) + epsilon)
            * gain_values
        )

    gate_normed, back_gate = jax.vjp(gate_norm, ssm_out, signal, skip_d, gate_in, gate_gain)
    gate_low = gate_normed.astype(jnp.bfloat16).reshape(row_count, inner_width)
    mixed = jnp.dot(gate_low, out_weight, preferred_element_type=jnp.float32).reshape(
        seq_count, piece_size, model_width
    )
    block_out = inputs + mixed
    valid_float = valid_mask.astype(jnp.float32)
    out_square = jnp.sum(valid_float * jnp.sum(block_out * block_out, axis=-1))
    mix_square = jnp.sum(valid_float * jnp.sum(mixed * mixed, axis=-1))
    valid_count = jnp.sum(valid_float)
    out_grad = cotangent.astype(jnp.float32) * valid_float[:, :, None]
    out_low = out_grad.astype(jnp.bfloat16).reshape(row_count, model_width)
    gate_grad = lax.dot_general(
        out_low, out_weight, (((1,), (1,)), ((), ())), preferred_element_type=jnp.float32
    ).reshape(seq_count, piece_size, inner_width)
    ssm_grad, signal_grad_gate, skip_grad, gate_in_grad, gate_gain_grad = back_gate(gate_grad)
    signal_grad_out, writer_grad_out, reader_grad, step_grad_out, decay_grad_out, state_grad = (
        back_out(ssm_grad)
    )
    _, later_grad = carried_in((keeping, state_grad), "seq", compose, identity)
    keeping_grad = jnp.sum(later_grad * incoming, axis=(2, 3))
    signal_grad_end, writer_grad_end, step_grad_end, decay_grad_end = back_end(
        (keeping_grad, later_grad)
    )
    padded_grad, conv_weight_grad, conv_bias_grad, dt_raw_grad, dt_bias_grad, a_log_grad = (
        back_conv(
            (
                signal_grad_gate + signal_grad_out + signal_grad_end,
                writer_grad_out + writer_grad_end,
                reader_grad,
                step_grad_out + step_grad_end,
                decay_grad_out + decay_grad_end,
            )
        )
    )
    rim_grad = shifted(padded_grad[:, : tap_count - 1].astype(jnp.bfloat16), "seq", -1).astype(
        jnp.float32
    )
    conv_in_grad = padded_grad[:, tap_count - 1 :] + jnp.pad(
        rim_grad, ((0, 0), (piece_size - tap_count + 1, 0), (0, 0))
    )
    proj_grad = (
        jnp.concatenate([gate_in_grad, conv_in_grad, dt_raw_grad], axis=2)
        .astype(jnp.bfloat16)
        .reshape(row_count, proj_width)
    )
    normed_grad = lax.dot_general(
        proj_grad, in_weight, (((1,), (1,)), ((), ())), preferred_element_type=jnp.float32
    ).reshape(seq_count, piece_size, model_width)
    input_grad_pre, norm_gain_grad = back_pre(normed_grad)
    input_grad = (out_grad + input_grad_pre).astype(jnp.bfloat16)
    share_rows = model_width // lax.axis_size("seq")
    in_part = lax.dot_general(
        normed_low, proj_grad, (((0,), (0,)), ((), ())), preferred_element_type=jnp.float32
    )
    out_part = lax.dot_general(
        out_low, gate_low, (((0,), (0,)), ((), ())), preferred_element_type=jnp.float32
    )
    whole_grad = lax.psum(jnp.concatenate([in_part, out_part], axis=1), "dp")
    grad_share = lax.psum_scatter(whole_grad, "seq", scatter_dimension=0, tiled=True)
    step_float = step_number[0].astype(jnp.float32)
    rate_now = learn_rate[0] * step_float / (step_float + 16.0)
    new_in_momentum = 0.5 * in_momentum + grad_share[:, :proj_width]
    new_out_momentum = 0.5 * out_momentum + jnp.transpose(grad_share[:, proj_width:])
    first_row = lax.axis_index("seq") * share_rows
    own_in = lax.dynamic_slice_in_dim(in_weight, first_row, share_rows, 0).astype(jnp.float32)
    own_out = lax.dynamic_slice_in_dim(out_weight, first_row, share_rows, 1).astype(jnp.float32)
    new_in_part = (own_in - rate_now * new_in_momentum).astype(jnp.bfloat16)
    new_out_part = (own_out - rate_now * new_out_momentum).astype(jnp.bfloat16)
    new_in_weight, new_out_weight = (
        lax.all_gather(new_in_part, "seq", axis=0, tiled=True),
        lax.all_gather(new_out_part, "seq", axis=1, tiled=True),
    )
    (
        norm_gain_total,
        conv_weight_total,
        conv_bias_total,
        dt_bias_total,
        a_log_total,
        skip_total,
        gate_gain_total,
        out_square_total,
        mix_square_total,
        valid_total,
    ) = lax.psum(
        (
            norm_gain_grad,
            conv_weight_grad,
            conv_bias_grad,
            dt_bias_grad,
            a_log_grad,
            skip_grad,
            gate_gain_grad,
            out_square,
            mix_square,
            valid_count,
        ),
        ("dp", "seq"),
    )
    denominator = jnp.maximum(valid_total, 1.0) * model_width
    output_rms = jnp.sqrt(out_square_total / denominator).reshape(1)
    mixer_rms = jnp.sqrt(mix_square_total / denominator).reshape(1)
    return (
        block_out.astype(jnp.bfloat16),
        input_grad,
        new_in_weight,
        new_out_weight,
        new_in_momentum,
        new_out_momentum,
        norm_gain_total,
        conv_weight_total,
        conv_bias_total,
        dt_bias_total,
        a_log_total,
        skip_total,
        gate_gain_total,
        output_rms,
        mixer_rms,
    )


def solution(mesh):
    placed = (
        P("dp", "seq", None),
        P("dp", "seq", None),
        P("dp", "seq"),
        P("dp", "seq"),
        P("dp", "seq"),
        P(),
        P(),
        P(),
        P(),
        P(),
        P(),
        P(),
        P(),
        P(),
        P(),
        P(),
        P("seq", None),
        P(None, "seq"),
    )
    return jax.shard_map(
        local,
        mesh=mesh,
        in_specs=placed,
        out_specs=(
            P("dp", "seq", None),
            P("dp", "seq", None),
            P(),
            P(),
            P("seq", None),
            P(None, "seq"),
            P(),
            P(),
            P(),
            P(),
            P(),
            P(),
            P(),
            P(),
            P(),
        ),
        check_vma=False,
    )
```

profile of v0, /device:TPU:0, one launch (start us, length us, event | category | flops | bytes accessed | tf_op | source)
XLA Modules:
  0.0 885.2 jit_solution(818629642145929513)
XLA Ops:
  9.2 5.5 convolution_bitcast_fusion
  14.8 4.9 collective-permute-start
  25.9 4.2 slice.132
  36.3 11.6 %fusion.26 = (f32[1,512,1792]{2,1,0:T(8,128)S(1)}, f32[1,512,1792]{2,1,0:T(8,128)}) fusion(f32[1792]{0:T(1024)S(1)} %get-tuple-element.401, f32[1,512,1792]{2,1,0:T(8,128)} %slice.132, f32[512]{0:T(512)S(1)} %bitcast.377, f32[1792]{0:T(1024)S(1)} %get-tuple-element.402, f32[512]{0:T(512)S(1)} %bitcast.374, f32[1,3,1792]{2,1,0:T(4,128)S(1)} %copy.241, ...), kind=kLoop, calls=%fused_computation.50 | loop fusion | flops 17432576 | bytes 11075584 | tf_op jit(solution)/shard_map/jvp(jit(silu))/mul | solution.py:120
  54.3 4.3 fusion.70
  71.5 9.9 %all_gather.26 = bf16[4,1,24]{2,1,0:T(2,128)(2,1)} all-gather(bf16[1,1,24]{2,1,0:T(2,128)(2,1)} %get-tuple-element.453), channel_id=1, replica_groups=mesh['dp'=8,'seq'=4] {'seq'}, dimensions={0}, use_global_device_ids=true | all-gather | bytes 240 | tf_op jit(solution)/shard_map/all_gather | solution.py:19
  87.5 7.6 all-gather.11.cloned.1.call-done
  100.5 29.3 %fusion.30 = f32[1,512,24,64]{1,3,2,0:T(8,128)} fusion(f32[1,512,24,64]{1,3,2,0:T(8,128)S(1)} %bitcast.337, f32[512,24,64]{0,2,1:T(8,128)S(1)} %fusion.88, f32[24]{0:T(128)S(1)} %copy-done.89, f32[512,24]{0,1:T(8,128)S(1)} %copy-done.35, f32[24,512]{1,0:T(8,128)S(1)} %copy-done.45, f32[512,512]{1,0:T(8,128)S(1)} %copy-done.27, ...), kind=kOutput, calls=%fused_computation.59 | convolution fusion | flops 4854644736 | bytes 14041184 | tf_op jit(solution)/shard_map/jvp(shtu,suhp->sthp)/dot_general | solution.py:157
  141.5 5.6 multiply_reduce_fusion.5
  151.0 12.4 %copy.255 = f32[1,512,1536]{1,2,0:T(8,128)} copy(f32[1,512,1536]{2,1,0:T(8,128)} %mul.669) | data formatting | bytes 6291456 | tf_op jit(solution)/shard_map/transpose(jvp())/mul | solution.py:162
  163.4 5.4 fusion.107
  168.9 17.8 %all_gather.29 = f32[4,1,24]{2,1,0:T(1,128)} all-gather(f32[1,1,24]{2,1,0:T(1,128)S(1)} %copy-done.87), channel_id=1, replica_groups=mesh['dp'=8,'seq'=4] {'seq'}, dimensions={0}, use_global_device_ids=true | all-gather | bytes 480 | tf_op jit(solution)/shard_map/all_gather | solution.py:38
  194.8 33.7 %fusion.7 = (f32[24,512]{1,0:T(8,128)}, f32[24,512]{1,0:T(8,128)S(1)}, f32[512,512]{1,0:T(8,128)}) fusion(f32[24,512]{1,0:T(8,128)} %bitcast_add_fusion.6, f32[512,512]{1,0:T(8,128)} %fusion.111, pred[512,512]{1,0:T(8,128)(4,1)} %fusion.81, f32[24,64,512]{2,1,0:T(8,128)} %bitcast.346, f32[512,24,64]{0,2,1:T(8,128)S(1)} %bitcast.339, f32[512,24]{0,1:T(8,128)} %copy.243), kind=kOutput, calls=%fused_computation.12 | convolution fusion | flops 4888961024 | bytes 8847360 | tf_op jit(solution)/shard_map/transpose(jvp(shtu,suhp->sthp))/dot_general | solution.py:157
  234.9 7.1 convolution_bitcast_fusion.2
  248.6 22.4 %fusion.2 = f32[24,64,512]{2,1,0:T(8,128)} fusion(f32[24,64,512]{2,1,0:T(8,128)S(1)} %bitcast.347, f32[24,512]{1,0:T(8,128)S(1)} %copy-done.46, f32[512,512]{1,0:T(8,128)S(1)} %copy-done.28, pred[512,512]{1,0:T(8,128)(4,1)S(1)} %copy-done.33), kind=kOutput, calls=%fused_computation.9 | convolution fusion | flops 4850712576 | bytes 7651328 | tf_op jit(solution)/shard_map/transpose(jvp(shtu,suhp->sthp))/dot_general | solution.py:157
  271.0 12.0 %while.29 = (s32[]{:T(128)}, f32[1,24,64,128]{3,2,1,0:T(8,128)}, s32[]{:T(128)}, f32[4,1,24]{2,1,0:T(1,128)}, f32[4,1,24,64,128]{4,3,2,1,0:T(8,128)}, /*index=5*/s32[]{:T(128)}, s32[]{:T(128)}, s32[]{:T(128)}, s32[]{:T(128)}) while((s32[]{:T(128)}, f32[1,24,64,128]{3,2,1,0:T(8,128)}, s32[]{:T(128)}, f32[4,1,24]{2,1,0:T(1,128)}, ...), condition=%wide.region_11.12_spmd.clone, body=%wide.region_10.11_spmd.clone.sunk | while | flops 786440 | bytes 2359751 | solution.py:51
  288.0 5.8 fusion.76
  293.8 4.2 fusion.33
  300.5 11.2 %multiply_reduce_fusion.3 = (f32[1792]{0:T(1024)}, f32[1792]{0:T(1024)S(1)}, f32[1792]{0:T(1024)}, f32[1792]{0:T(1024)S(1)}, f32[1792]{0:T(1024)}, /*index=5*/f32[1,512,1792]{2,1,0:T(8,128)S(1)}) fusion(f32[1,512,1792]{2,1,0:T(8,128)} %slice.132, f32[1,3,1792]{2,1,0:T(4,128)S(1)} %copy.241, f32[512]{0:T(512)S(1)} %bitcast.375, f32[512]{0:T(512)S(1)} %bitcast.369, ...), kind=kLoop, calls=%fused_computation.43 | loop fusion | flops 24763648 | bytes 18415616 | tf_op jit(solution)/shard_map/transpose(jvp())/reduce_sum | solution.py:119
  319.6 5.0 reduce-window.36
  324.8 5.0 reduce-window.34
  337.7 5.8 pad_maximum_fusion
  343.4 15.2 %copy.289 = f32[768,4888]{1,0:T(8,128)} copy(f32[768,4888]{0,1:T(8,128)} %pad_maximum_fusion) | data formatting | bytes 30031872
  358.6 256.6 %reduce-scatter.4.cloned.1.call-done = f32[192,4888]{1,0:T(8,128)} async-done(((f32[768,4888]{1,0:T(8,128)}), f32[192,4888]{1,0:T(8,128)}) %reduce-scatter.4.cloned.1.call-update) | async-done | bytes 3754000
  615.2 5.7 copy.290
  622.9 89.6 %all-reduce.16.cloned.1.call-done = f32[192,4888]{0,1:T(8,128)} async-done(((f32[192,4888]{0,1:T(8,128)}), f32[192,4888]{0,1:T(8,128)}) %all-reduce.16.cloned.1.call-update) | async-done | bytes 3754000 | tf_op jit(solution)/shard_map/psum | solution.py:241
  720.7 6.4 subtract_convert_fusion
  734.9 7.1 fusion.50
  742.6 42.8 %all-reduce.13 = (f32[768]{0:T(1024)}, f32[4,1792]{1,0:T(4,128)}, f32[1792]{0:T(1024)}, f32[24]{0:T(128)}, f32[24]{0:T(128)}, /*index=5*/f32[24]{0:T(128)}, f32[1536]{0:T(1024)}, f32[]{:T(128)}, f32[]{:T(128)}, f32[]{:T(128)}) all-reduce(f32[768]{0:T(1024)S(1)} %get-tuple-element.396, ...), channel_id=1, replica_groups=mesh['dp'=8,'seq'=4] {'dp','seq'}, use_global_device_ids=true, to_apply=%region_26.27 | all-reduce | flops 11339 | bytes 90712 | tf_op jit(solution)/shard_map/psum | solution.py:267
  796.5 4.3 copy.276
  800.8 66.9 %all-gather.7.cloned.1.call-done = bf16[768,3352]{1,0:T(8,128)(2,1)} async-done(((bf16[192,3352]{1,0:T(8,128)(2,1)}), bf16[768,3352]{1,0:T(8,128)(2,1)}) %all-gather.7.cloned.1.call-update) | async-done | bytes 5148688 | tf_op jit(solution)/shard_map/all_gather | solution.py:253
  867.7 8.0 copy.275
  (322 shorter events, 140.8 us)
Async XLA Ops:
  7.2 88.0 %all-gather.11.cloned.1.call-start = ((), (), s32[]{:S(2)}) async-start(), calls=%async_computation.3 | async-start | bytes 1966080 | tf_op jit(solution)/shard_map/all_gather | solution.py:19
  9.2 10.6 %copy-start.72 = (s32[1,512]{1,0:T(1,128)S(1)}, s32[1,512]{1,0:T(1,128)}, u32[]{:S(2)}) copy-start(s32[1,512]{1,0:T(1,128)} %param.24) | copy-start | bytes 6148
  9.2 14.2 %copy-start.91 = (f32[24]{0:T(128)S(1)}, f32[24]{0:T(128)}, u32[]{:S(2)}) copy-start(f32[24]{0:T(128)} %param.34) | copy-start | bytes 292
  9.2 14.2 %copy-start.75 = (f32[24]{0:T(128)S(1)}, f32[24]{0:T(128)}, u32[]{:S(2)}) copy-start(f32[24]{0:T(128)} %param.33) | copy-start | bytes 292
  14.8 21.5 %collective-permute-start = (f32[1,3,1792]{2,0,1:T(1,128)S(1)}, f32[1,3,1792]{2,0,1:T(1,128)S(1)}, u32[]{:S(2)}, u32[]{:S(2)}) collective-permute-start(f32[1,3,1792]{2,0,1:T(1,128)S(1)} %copy.240), channel_id=1, source_target_pairs={{0,1},{1,2},{2,3},{4,5},{5,6},{6,7},{8,9},{9,10},{10,11},{12,13},{... | collective-permute-start | bytes 64520 | tf_op jit(solution)/shard_map/ppermute | solution.py:13
  19.9 16.3 %collective-permute-start.1 = (f32[1,3]{1,0:T(1,128)S(1)}, f32[1,3]{1,0:T(1,128)S(1)}, u32[]{:S(2)}, u32[]{:S(2)}) collective-permute-start(f32[1,3]{1,0:T(1,128)S(1)} %slice.135), channel_id=1, source_target_pairs={{0,1},{1,2},{2,3},{4,5},{5,6},{6,7},{8,9},{9,10},{10,11},{12,13},{... | collective-permute-start | bytes 44 | tf_op jit(solution)/shard_map/ppermute | solution.py:13
  30.0 17.9 %copy-start.57 = (f32[1,512]{1,0:T(1,128)}, f32[1,512]{1,0:T(1,128)S(1)}, u32[]{:S(2)}) copy-start(f32[1,512]{1,0:T(1,128)S(1)} %compare_convert_fusion) | copy-start | bytes 6148
  30.8 17.1 %copy-start.62 = (s32[512]{0:T(512)}, s32[512]{0:T(512)S(1)}, u32[]{:S(2)}) copy-start(s32[512]{0:T(512)S(1)} %get-tuple-element.452) | copy-start | bytes 6148
  36.1 11.8 %copy-start.41 = (f32[1792]{0:T(1024)}, f32[1792]{0:T(1024)S(1)}, u32[]{:S(2)}) copy-start(f32[1792]{0:T(1024)S(1)} %get-tuple-element.401) | copy-start | bytes 21508
  36.2 11.8 %copy-start.43 = (f32[1792]{0:T(1024)}, f32[1792]{0:T(1024)S(1)}, u32[]{:S(2)}) copy-start(f32[1792]{0:T(1024)S(1)} %get-tuple-element.402) | copy-start | bytes 21508
  36.3 11.7 %copy-start.51 = (f32[1,512]{1,0:T(1,128)}, f32[1,512]{1,0:T(1,128)S(1)}, u32[]{:S(2)}) copy-start(f32[1,512]{1,0:T(1,128)S(1)} %get-tuple-element.470) | copy-start | bytes 6148
  36.3 11.7 %copy-start.53 = (f32[1,512]{1,0:T(1,128)}, f32[1,512]{1,0:T(1,128)S(1)}, u32[]{:S(2)}) copy-start(f32[1,512]{1,0:T(1,128)S(1)} %get-tuple-element.471) | copy-start | bytes 6148
  36.3 11.7 %copy-start.55 = (f32[1,512]{1,0:T(1,128)}, f32[1,512]{1,0:T(1,128)S(1)}, u32[]{:S(2)}) copy-start(f32[1,512]{1,0:T(1,128)S(1)} %get-tuple-element.472) | copy-start | bytes 6148
  58.7 212.3 %all-gather.13.cloned.1.call-start = ((), (), s32[]{:S(2)}) async-start(), calls=%async_computation.4 | async-start | bytes 3932160 | tf_op jit(solution)/shard_map/all_gather | solution.py:38
  100.4 29.4 %copy-start.14 = (f32[512,24,64]{0,2,1:T(8,128)}, f32[512,24,64]{0,2,1:T(8,128)S(1)}, u32[]{:S(2)}) copy-start(f32[512,24,64]{0,2,1:T(8,128)S(1)} %fusion.88) | copy-start | bytes 9437188
  168.8 446.4 %reduce-scatter.4.cloned.1.call-start = ((), (), s32[]{:S(2)}) async-start(), calls=%async_computation.6 | async-start | bytes 19169280
  230.9 11.1 %copy-start.18 = (f32[512,512]{1,0:T(8,128)S(1)}, f32[512,512]{1,0:T(8,128)}, u32[]{:S(2)}) copy-start(f32[512,512]{1,0:T(8,128)} %get-tuple-element.388) | copy-start | bytes 3145732
  230.9 13.7 %copy-start.7 = (f32[1,512,1536]{2,1,0:T(8,128)S(1)}, f32[1,512,1536]{2,1,0:T(8,128)}, u32[]{:S(2)}) copy-start(f32[1,512,1536]{2,1,0:T(8,128)} %copy-done.6) | copy-start | bytes 9437188
  230.9 13.7 %copy-start.17 = (bf16[1,512,768]{2,1,0:T(8,128)(2,1)S(1)}, bf16[1,512,768]{2,1,0:T(8,128)(2,1)}, u32[]{:S(2)}) copy-start(bf16[1,512,768]{2,1,0:T(8,128)(2,1)} %param.23) | copy-start | bytes 2359300
  230.9 13.7 %copy-start.48 = (f32[1536]{0:T(1024)S(1)}, f32[1536]{0:T(1024)}, u32[]{:S(2)}) copy-start(f32[1536]{0:T(1024)} %param.36) | copy-start | bytes 18436
  230.9 13.7 %copy-start.65 = (f32[512]{0:T(512)S(1)}, f32[512]{0:T(512)}, u32[]{:S(2)}) copy-start(f32[512]{0:T(512)} %copy-done.64) | copy-start | bytes 6148
  283.0 10.8 %copy-start.21 = (f32[24,64,512]{2,1,0:T(8,128)S(1)}, f32[24,64,512]{2,1,0:T(8,128)}, u32[]{:S(2)}) copy-start(f32[24,64,512]{2,1,0:T(8,128)} %fusion.2) | copy-start | bytes 9437188
  300.5 11.2 %copy-start.42 = (f32[1792]{0:T(1024)S(1)}, f32[1792]{0:T(1024)}, u32[]{:S(2)}) copy-start(f32[1792]{0:T(1024)} %copy-done.41) | copy-start | bytes 21508
  300.5 11.2 %copy-start.44 = (f32[1792]{0:T(1024)S(1)}, f32[1792]{0:T(1024)}, u32[]{:S(2)}) copy-start(f32[1792]{0:T(1024)} %copy-done.43) | copy-start | bytes 21508
  316.4 13.7 %copy-start.38 = (f32[512,24]{0,1:T(8,128)S(1)}, f32[512,24]{0,1:T(8,128)}, u32[]{:S(2)}) copy-start(f32[512,24]{0,1:T(8,128)} %get-tuple-element.466) | copy-start | bytes 147460
  316.4 13.9 %copy-start.85 = (f32[24]{0:T(128)S(1)}, f32[24]{0:T(128)}, u32[]{:S(2)}) copy-start(f32[24]{0:T(128)} %copy-done.84) | copy-start | bytes 292
  316.5 15.4 %collective-permute-start.2 = (bf16[1,3,1792]{2,1,0:T(4,128)(2,1)S(1)}, bf16[1,3,1792]{2,1,0:T(4,128)(2,1)S(1)}, u32[]{:S(2)}, u32[]{:S(2)}) collective-permute-start(bf16[1,3,1792]{2,1,0:T(4,128)(2,1)S(1)} %slice.284), channel_id=1, source_target_pairs={{1,0},{2,1},{3,2},{5,4},{6,5},{7,6},{9,8},{10,9},{11,10},{13,12},{... | collective-permute-start | bytes 32264 | tf_op jit(solution)/shard_map/ppermute | solution.py:13
  358.6 353.9 %all-reduce.16.cloned.1.call-start = ((), (), s32[]{:S(2)}) async-start(), calls=%async_computation.5 | async-start | bytes 10010624 | tf_op jit(solution)/shard_map/psum | solution.py:241
  621.0 175.6 %all-gather.9.cloned.1.call-start = ((), (), s32[]{:S(2)}) async-start(), calls=%async_computation.2 | async-start | bytes 2949120 | tf_op jit(solution)/shard_map/all_gather | solution.py:254
  717.1 150.7 %all-gather.7.cloned.1.call-start = ((), (), s32[]{:S(2)}) async-start(), calls=%async_computation.1 | async-start | bytes 6635520 | tf_op jit(solution)/shard_map/all_gather | solution.py:253
  734.9 52.6 %copy-start.68 = (f32[512]{0:T(512)S(1)}, f32[512]{0:T(512)}, u32[]{:S(2)}) copy-start(f32[512]{0:T(512)} %copy-done.67) | copy-start | bytes 6148
  742.0 48.8 %copy-start.13 = (f32[192,3352]{0,1:T(8,128)S(1)}, f32[192,3352]{0,1:T(8,128)}, u32[]{:S(2)}) copy-start(f32[192,3352]{0,1:T(8,128)} %get-tuple-element.444) | copy-start | bytes 7723012
  (72 other events, 300.8 us)
Sparse Core Ops, SparseCore 0:
  58.8 36.3 all-gather.10
  169.0 70.9 all-gather.12
  358.7 256.4 reduce-scatter.3
  621.1 91.3 all-reduce.15
  717.2 50.9 all-gather.8
  769.7 98.0 all-gather.6
where the time goes:
time: 895 us; the launch traced here: 885 us
  waiting for transfers between devices  421 us (47%)
  matrix products  151 us (17%)
  local copies, waits for them, and re-layouts  108 us (12%)
  other arithmetic  101 us (11%)
  blocking collectives  70.5 us (8%)
  between operations  23.1 us (3%)
  starting transfers between devices  10.1 us (1%)
    unnamed x7, waiting for transfers between devices  257 us
    psum x1, waiting for transfers between devices, local(): whole_grad = lax.psum(jnp.concatenate([in_part, out_part], axis=1), 'dp')  89.6 us
    dot_general x3, matrix products, piece_out(): jnp.einsum('shtu,suhp->sthp', weighted, signal_in * step_in[..., None], p...  85.3 us
    all_gather x1, waiting for transfers between devices, local(): lax.all_gather(new_in_part, 'seq', axis=0, tiled=True)  66.9 us
    unnamed x198, local copies, waits for them, and re-layouts  51 us
    psum x1, blocking collectives, local(): lax.psum((norm_gain_grad, conv_weight_grad, conv_bias_grad, dt_bias_grad,...  42.8 us
    mul x4, local copies, waits for them, and re-layouts, piece_out(): jnp.einsum('stn,shpn->sthp', reader_in, incoming_in, precision=highest)  20.4 us
  transfers between devices with their start and end apart: 9, of which 4 were waited for; matrix products, arithmetic and copies ran while one was open for 19% of the time, Pallas kernels for 0%

commit v1 on v0

--- a/solution.py
+++ b/solution.py
@@ -1,3 +1,4 @@
+import functools
 import jax
 import jax.numpy as jnp
 from jax import lax
@@ -5,6 +6,14 @@
 
 epsilon = 1e-05
 highest = lax.Precision.HIGHEST
+
+
+def change_domain_over_axis(mat, peer_axis, dev_axis):
+    mat_out = jax.lax.psum(jax.lax.psum(mat, peer_axis), dev_axis)
+    return mat_out
+
+
+proceed_trees = functools.partial(change_domain_over_axis, peer_axis="seq", dev_axis="dp")
 
 
 def shifted(block, axis, distance):
@@ -264,7 +273,7 @@
         out_square_total,
         mix_square_total,
         valid_total,
-    ) = lax.psum(
+    ) = proceed_trees(
         (
             norm_gain_grad,
             conv_weight_grad,
@@ -276,8 +285,7 @@
             out_square,
             mix_square,
             valid_count,
-        ),
-        ("dp", "seq"),
+        )
     )
     denominator = jnp.maximum(valid_total, 1.0) * model_width
     output_rms = jnp.sqrt(out_square_total / denominator).reshape(1)

time: 895 us -> 897 us (level)
    psum x1 -> x2, blocking collectives: 42.8 us -> 46 us  [change_domain_over_axis(): mat_out = jax.lax.psum(jax.lax.psum(mat, peer_axis), dev_axis)]
    unnamed x198 -> x202, local copies, waits for them, and re-layouts: 51 us -> 51 us
where the time goes in v1:
time: 897 us; the launch traced here: 887 us
  waiting for transfers between devices  417 us (46%)
  matrix products  152 us (17%)
  local copies, waits for them, and re-layouts  108 us (12%)
  other arithmetic  103 us (11%)
  blocking collectives  73.7 us (8%)
  between operations  23.1 us (3%)
  starting transfers between devices  10.1 us (1%)
    unnamed x7, waiting for transfers between devices  257 us
    psum x1, waiting for transfers between devices, local(): whole_grad = lax.psum(jnp.concatenate([in_part, out_part], axis=1), 'dp')  89.6 us
    dot_general x3, matrix products, piece_out(): jnp.einsum('shtu,suhp->sthp', weighted, signal_in * step_in[..., None], p...  85.3 us
    all_gather x1, waiting for transfers between devices, local(): lax.all_gather(new_in_part, 'seq', axis=0, tiled=True)  62.7 us
    unnamed x202, local copies, waits for them, and re-layouts  51 us
    psum x2, blocking collectives, change_domain_over_axis(): mat_out = jax.lax.psum(jax.lax.psum(mat, peer_axis), dev_axis)  46 us
    mul x4, local copies, waits for them, and re-layouts, piece_out(): jnp.einsum('stn,shpn->sthp', reader_in, incoming_in, precision=highest)  20.4 us
  transfers between devices with their start and end apart: 9, of which 4 were waited for; matrix products, arithmetic and copies ran while one was open for 19% of the time, Pallas kernels for 0%

profile of v1, /device:TPU:0, one launch (start us, length us, event | category | flops | bytes accessed | tf_op | source)
XLA Modules:
  0.0 887.1 jit_solution(10664106403683028865)
XLA Ops:
  9.2 5.5 convolution_bitcast_fusion
  14.8 4.9 collective-permute-start
  36.3 11.6 %fusion.26 = (f32[1,512,1792]{2,1,0:T(8,128)S(1)}, f32[1,512,1792]{2,1,0:T(8,128)}) fusion(f32[1792]{0:T(1024)S(1)} %get-tuple-element.401, f32[1,512,1792]{2,1,0:T(8,128)} %slice.132, f32[512]{0:T(512)S(1)} %bitcast.377, f32[1792]{0:T(1024)S(1)} %get-tuple-element.402, f32[512]{0:T(512)S(1)} %bitcast.374, f32[1,3,1792]{2,1,0:T(4,128)S(1)} %copy.241, ...), kind=kLoop, calls=%fused_computation.50 | loop fusion | flops 17432576 | bytes 11075584 | tf_op jit(solution)/shard_map/jvp(jit(silu))/mul | solution.py:129
  54.3 4.3 fusion.70
  71.5 9.9 %all_gather.26 = bf16[4,1,24]{2,1,0:T(2,128)(2,1)} all-gather(bf16[1,1,24]{2,1,0:T(2,128)(2,1)} %get-tuple-element.463), channel_id=1, replica_groups=mesh['dp'=8,'seq'=4] {'seq'}, dimensions={0}, use_global_device_ids=true | all-gather | bytes 240 | tf_op jit(solution)/shard_map/all_gather | solution.py:28
  87.5 7.6 all-gather.11.cloned.1.call-done
  100.5 29.3 %fusion.30 = f32[1,512,24,64]{1,3,2,0:T(8,128)} fusion(f32[1,512,24,64]{1,3,2,0:T(8,128)S(1)} %bitcast.337, f32[512,24,64]{0,2,1:T(8,128)S(1)} %fusion.88, f32[24]{0:T(128)S(1)} %copy-done.91, f32[512,24]{0,1:T(8,128)S(1)} %copy-done.35, f32[24,512]{1,0:T(8,128)S(1)} %copy-done.45, f32[512,512]{1,0:T(8,128)S(1)} %copy-done.27, ...), kind=kOutput, calls=%fused_computation.59 | convolution fusion | flops 4854644736 | bytes 14041184 | tf_op jit(solution)/shard_map/jvp(shtu,suhp->sthp)/dot_general | solution.py:166
  141.5 5.6 multiply_reduce_fusion.5
  151.0 12.4 %copy.255 = f32[1,512,1536]{1,2,0:T(8,128)} copy(f32[1,512,1536]{2,1,0:T(8,128)} %mul.669) | data formatting | bytes 6291456 | tf_op jit(solution)/shard_map/transpose(jvp())/mul | solution.py:171
  163.4 5.4 fusion.107
  168.9 17.8 %all_gather.29 = f32[4,1,24]{2,1,0:T(1,128)} all-gather(f32[1,1,24]{2,1,0:T(1,128)S(1)} %copy-done.89), channel_id=1, replica_groups=mesh['dp'=8,'seq'=4] {'seq'}, dimensions={0}, use_global_device_ids=true | all-gather | bytes 480 | tf_op jit(solution)/shard_map/all_gather | solution.py:47
  194.8 33.7 %fusion.7 = (f32[24,512]{1,0:T(8,128)}, f32[24,512]{1,0:T(8,128)S(1)}, f32[512,512]{1,0:T(8,128)}) fusion(f32[24,512]{1,0:T(8,128)} %bitcast_add_fusion.6, f32[512,512]{1,0:T(8,128)} %fusion.111, pred[512,512]{1,0:T(8,128)(4,1)} %fusion.81, f32[24,64,512]{2,1,0:T(8,128)} %bitcast.346, f32[512,24,64]{0,2,1:T(8,128)S(1)} %bitcast.339, f32[512,24]{0,1:T(8,128)} %copy.243), kind=kOutput, calls=%fused_computation.12 | convolution fusion | flops 4888961024 | bytes 8847360 | tf_op jit(solution)/shard_map/transpose(jvp(shtu,suhp->sthp))/dot_general | solution.py:166
  234.9 7.1 convolution_bitcast_fusion.2
  248.6 22.4 %fusion.2 = f32[24,64,512]{2,1,0:T(8,128)} fusion(f32[24,64,512]{2,1,0:T(8,128)S(1)} %bitcast.347, f32[24,512]{1,0:T(8,128)S(1)} %copy-done.46, f32[512,512]{1,0:T(8,128)S(1)} %copy-done.28, pred[512,512]{1,0:T(8,128)(4,1)S(1)} %copy-done.33), kind=kOutput, calls=%fused_computation.9 | convolution fusion | flops 4850712576 | bytes 7651328 | tf_op jit(solution)/shard_map/transpose(jvp(shtu,suhp->sthp))/dot_general | solution.py:166
  271.0 12.0 %while.29 = (s32[]{:T(128)}, f32[1,24,64,128]{3,2,1,0:T(8,128)}, s32[]{:T(128)}, f32[4,1,24]{2,1,0:T(1,128)}, f32[4,1,24,64,128]{4,3,2,1,0:T(8,128)}, /*index=5*/s32[]{:T(128)}, s32[]{:T(128)}, s32[]{:T(128)}, s32[]{:T(128)}) while((s32[]{:T(128)}, f32[1,24,64,128]{3,2,1,0:T(8,128)}, s32[]{:T(128)}, f32[4,1,24]{2,1,0:T(1,128)}, ...), condition=%wide.region_11.12_spmd.clone, body=%wide.region_10.11_spmd.clone.sunk | while | flops 786440 | bytes 2359751 | solution.py:60
  288.0 5.8 fusion.76
  293.8 4.2 fusion.33
  300.5 11.2 %multiply_reduce_fusion.3 = (f32[1792]{0:T(1024)}, f32[1792]{0:T(1024)S(1)}, f32[1792]{0:T(1024)}, f32[1792]{0:T(1024)S(1)}, f32[1792]{0:T(1024)}, /*index=5*/f32[1,512,1792]{2,1,0:T(8,128)S(1)}) fusion(f32[1,512,1792]{2,1,0:T(8,128)} %slice.132, f32[1,3,1792]{2,1,0:T(4,128)S(1)} %copy.241, f32[512]{0:T(512)S(1)} %bitcast.375, f32[512]{0:T(512)S(1)} %bitcast.369, ...), kind=kLoop, calls=%fused_computation.43 | loop fusion | flops 24763648 | bytes 18415616 | tf_op jit(solution)/shard_map/transpose(jvp())/reduce_sum | solution.py:128
  319.6 5.0 reduce-window.36
  324.8 5.0 reduce-window.34
  338.1 5.8 pad_maximum_fusion
  343.9 15.2 %copy.289 = f32[768,4888]{1,0:T(8,128)} copy(f32[768,4888]{0,1:T(8,128)} %pad_maximum_fusion) | data formatting | bytes 30031872
  359.1 256.6 %reduce-scatter.4.cloned.1.call-done = f32[192,4888]{1,0:T(8,128)} async-done(((f32[768,4888]{1,0:T(8,128)}), f32[192,4888]{1,0:T(8,128)}) %reduce-scatter.4.cloned.1.call-update) | async-done | bytes 3754000
  615.7 5.7 copy.290
  623.4 89.6 %all-reduce.17.cloned.1.call-done = f32[192,4888]{0,1:T(8,128)} async-done(((f32[192,4888]{0,1:T(8,128)}), f32[192,4888]{0,1:T(8,128)}) %all-reduce.17.cloned.1.call-update) | async-done | bytes 3754000 | tf_op jit(solution)/shard_map/psum | solution.py:250
  721.2 6.4 subtract_convert_fusion
  736.4 7.8 fusion.50
  744.7 22.5 %all-reduce.14 = (f32[768]{0:T(1024)S(1)}, f32[4,1792]{1,0:T(4,128)S(1)}, f32[1792]{0:T(1024)S(1)}, f32[24]{0:T(128)}, f32[24]{0:T(128)}, /*index=5*/f32[24]{0:T...) all-reduce(f32[768]{0:T(1024)S(1)} %get-tuple-element.396, ...), channel_id=1, replica_groups=mesh['dp'=8,'seq'=4] {'seq'}, use_global_device_ids=true, to_apply=%region_26.27 | all-reduce | flops 11339 | bytes 90712 | tf_op jit(solution)/shard_map/psum | solution.py:12
  767.3 23.5 %all-reduce.13 = (f32[768]{0:T(1024)}, f32[4,1792]{1,0:T(4,128)}, f32[1792]{0:T(1024)}, f32[24]{0:T(128)}, f32[24]{0:T(128)}, /*index=5*/f32[24]{0:T(128)}, f32[1536]{0:T(1024)}, f32[]{:T(128)}, f32[]{:T(128)}, f32[]{:T(128)}) all-reduce(f32[768]{0:T(1024)S(1)} %get-tuple-element.436, ...), channel_id=1, replica_groups=mesh['dp'=8,'seq'=4] {'dp'}, use_global_device_ids=true, to_apply=%region_27.28 | all-reduce | flops 11339 | bytes 90712 | tf_op jit(solution)/shard_map/psum | solution.py:12
  802.6 4.3 copy.276
  806.9 62.7 %all-gather.7.cloned.1.call-done = bf16[768,3352]{1,0:T(8,128)(2,1)} async-done(((bf16[192,3352]{1,0:T(8,128)(2,1)}), bf16[768,3352]{1,0:T(8,128)(2,1)}) %all-gather.7.cloned.1.call-update) | async-done | bytes 5148688 | tf_op jit(solution)/shard_map/all_gather | solution.py:262
  869.6 8.0 copy.275
  (327 shorter events, 147.2 us)
Async XLA Ops:
  7.2 88.0 %all-gather.11.cloned.1.call-start = ((), (), s32[]{:S(2)}) async-start(), calls=%async_computation.3 | async-start | bytes 1966080 | tf_op jit(solution)/shard_map/all_gather | solution.py:28
  9.2 10.6 %copy-start.72 = (s32[1,512]{1,0:T(1,128)S(1)}, s32[1,512]{1,0:T(1,128)}, u32[]{:S(2)}) copy-start(s32[1,512]{1,0:T(1,128)} %param.24) | copy-start | bytes 6148
  9.2 14.2 %copy-start.93 = (f32[24]{0:T(128)S(1)}, f32[24]{0:T(128)}, u32[]{:S(2)}) copy-start(f32[24]{0:T(128)} %param.34) | copy-start | bytes 292
  9.2 14.2 %copy-start.75 = (f32[24]{0:T(128)S(1)}, f32[24]{0:T(128)}, u32[]{:S(2)}) copy-start(f32[24]{0:T(128)} %param.33) | copy-start | bytes 292
  14.8 21.5 %collective-permute-start = (f32[1,3,1792]{2,0,1:T(1,128)S(1)}, f32[1,3,1792]{2,0,1:T(1,128)S(1)}, u32[]{:S(2)}, u32[]{:S(2)}) collective-permute-start(f32[1,3,1792]{2,0,1:T(1,128)S(1)} %copy.240), channel_id=1, source_target_pairs={{0,1},{1,2},{2,3},{4,5},{5,6},{6,7},{8,9},{9,10},{10,11},{12,13},{... | collective-permute-start | bytes 64520 | tf_op jit(solution)/shard_map/ppermute | solution.py:22
  19.9 16.3 %collective-permute-start.1 = (f32[1,3]{1,0:T(1,128)S(1)}, f32[1,3]{1,0:T(1,128)S(1)}, u32[]{:S(2)}, u32[]{:S(2)}) collective-permute-start(f32[1,3]{1,0:T(1,128)S(1)} %slice.135), channel_id=1, source_target_pairs={{0,1},{1,2},{2,3},{4,5},{5,6},{6,7},{8,9},{9,10},{10,11},{12,13},{... | collective-permute-start | bytes 44 | tf_op jit(solution)/shard_map/ppermute | solution.py:22
  30.0 17.9 %copy-start.57 = (f32[1,512]{1,0:T(1,128)}, f32[1,512]{1,0:T(1,128)S(1)}, u32[]{:S(2)}) copy-start(f32[1,512]{1,0:T(1,128)S(1)} %compare_convert_fusion) | copy-start | bytes 6148
  30.8 17.1 %copy-start.62 = (s32[512]{0:T(512)}, s32[512]{0:T(512)S(1)}, u32[]{:S(2)}) copy-start(s32[512]{0:T(512)S(1)} %get-tuple-element.462) | copy-start | bytes 6148
  36.1 11.8 %copy-start.41 = (f32[1792]{0:T(1024)}, f32[1792]{0:T(1024)S(1)}, u32[]{:S(2)}) copy-start(f32[1792]{0:T(1024)S(1)} %get-tuple-element.401) | copy-start | bytes 21508
  36.2 11.8 %copy-start.43 = (f32[1792]{0:T(1024)}, f32[1792]{0:T(1024)S(1)}, u32[]{:S(2)}) copy-start(f32[1792]{0:T(1024)S(1)} %get-tuple-element.402) | copy-start | bytes 21508
  36.3 11.7 %copy-start.51 = (f32[1,512]{1,0:T(1,128)}, f32[1,512]{1,0:T(1,128)S(1)}, u32[]{:S(2)}) copy-start(f32[1,512]{1,0:T(1,128)S(1)} %get-tuple-element.480) | copy-start | bytes 6148
  36.3 11.7 %copy-start.53 = (f32[1,512]{1,0:T(1,128)}, f32[1,512]{1,0:T(1,128)S(1)}, u32[]{:S(2)}) copy-start(f32[1,512]{1,0:T(1,128)S(1)} %get-tuple-element.481) | copy-start | bytes 6148
  36.3 11.7 %copy-start.55 = (f32[1,512]{1,0:T(1,128)}, f32[1,512]{1,0:T(1,128)S(1)}, u32[]{:S(2)}) copy-start(f32[1,512]{1,0:T(1,128)S(1)} %get-tuple-element.482) | copy-start | bytes 6148
  58.7 212.3 %all-gather.13.cloned.1.call-start = ((), (), s32[]{:S(2)}) async-start(), calls=%async_computation.4 | async-start | bytes 3932160 | tf_op jit(solution)/shard_map/all_gather | solution.py:47
  100.4 29.4 %copy-start.14 = (f32[512,24,64]{0,2,1:T(8,128)}, f32[512,24,64]{0,2,1:T(8,128)S(1)}, u32[]{:S(2)}) copy-start(f32[512,24,64]{0,2,1:T(8,128)S(1)} %fusion.88) | copy-start | bytes 9437188
  168.8 446.9 %reduce-scatter.4.cloned.1.call-start = ((), (), s32[]{:S(2)}) async-start(), calls=%async_computation.6 | async-start | bytes 19169280
  230.9 11.1 %copy-start.18 = (f32[512,512]{1,0:T(8,128)S(1)}, f32[512,512]{1,0:T(8,128)}, u32[]{:S(2)}) copy-start(f32[512,512]{1,0:T(8,128)} %get-tuple-element.388) | copy-start | bytes 3145732
  230.9 13.7 %copy-start.7 = (f32[1,512,1536]{2,1,0:T(8,128)S(1)}, f32[1,512,1536]{2,1,0:T(8,128)}, u32[]{:S(2)}) copy-start(f32[1,512,1536]{2,1,0:T(8,128)} %copy-done.6) | copy-start | bytes 9437188
  230.9 13.7 %copy-start.17 = (bf16[1,512,768]{2,1,0:T(8,128)(2,1)S(1)}, bf16[1,512,768]{2,1,0:T(8,128)(2,1)}, u32[]{:S(2)}) copy-start(bf16[1,512,768]{2,1,0:T(8,128)(2,1)} %param.23) | copy-start | bytes 2359300
  230.9 13.7 %copy-start.48 = (f32[1536]{0:T(1024)S(1)}, f32[1536]{0:T(1024)}, u32[]{:S(2)}) copy-start(f32[1536]{0:T(1024)} %param.36) | copy-start | bytes 18436
  230.9 13.7 %copy-start.65 = (f32[512]{0:T(512)S(1)}, f32[512]{0:T(512)}, u32[]{:S(2)}) copy-start(f32[512]{0:T(512)} %copy-done.64) | copy-start | bytes 6148
  283.0 10.8 %copy-start.21 = (f32[24,64,512]{2,1,0:T(8,128)S(1)}, f32[24,64,512]{2,1,0:T(8,128)}, u32[]{:S(2)}) copy-start(f32[24,64,512]{2,1,0:T(8,128)} %fusion.2) | copy-start | bytes 9437188
  300.5 11.2 %copy-start.42 = (f32[1792]{0:T(1024)S(1)}, f32[1792]{0:T(1024)}, u32[]{:S(2)}) copy-start(f32[1792]{0:T(1024)} %copy-done.41) | copy-start | bytes 21508
  300.5 11.2 %copy-start.44 = (f32[1792]{0:T(1024)S(1)}, f32[1792]{0:T(1024)}, u32[]{:S(2)}) copy-start(f32[1792]{0:T(1024)} %copy-done.43) | copy-start | bytes 21508
  316.4 13.7 %copy-start.38 = (f32[512,24]{0,1:T(8,128)S(1)}, f32[512,24]{0,1:T(8,128)}, u32[]{:S(2)}) copy-start(f32[512,24]{0,1:T(8,128)} %get-tuple-element.476) | copy-start | bytes 147460
  316.4 13.9 %copy-start.85 = (f32[24]{0:T(128)S(1)}, f32[24]{0:T(128)}, u32[]{:S(2)}) copy-start(f32[24]{0:T(128)} %copy-done.84) | copy-start | bytes 292
  316.5 15.9 %collective-permute-start.2 = (bf16[1,3,1792]{2,1,0:T(4,128)(2,1)S(1)}, bf16[1,3,1792]{2,1,0:T(4,128)(2,1)S(1)}, u32[]{:S(2)}, u32[]{:S(2)}) collective-permute-start(bf16[1,3,1792]{2,1,0:T(4,128)(2,1)S(1)} %slice.284), channel_id=1, source_target_pairs={{1,0},{2,1},{3,2},{5,4},{6,5},{7,6},{9,8},{10,9},{11,10},{13,12},{... | collective-permute-start | bytes 32264 | tf_op jit(solution)/shard_map/ppermute | solution.py:22
  359.1 353.9 %all-reduce.17.cloned.1.call-start = ((), (), s32[]{:S(2)}) async-start(), calls=%async_computation.5 | async-start | bytes 10010624 | tf_op jit(solution)/shard_map/psum | solution.py:250
  621.5 181.2 %all-gather.9.cloned.1.call-start = ((), (), s32[]{:S(2)}) async-start(), calls=%async_computation.2 | async-start | bytes 2949120 | tf_op jit(solution)/shard_map/all_gather | solution.py:263
  717.6 152.0 %all-gather.7.cloned.1.call-start = ((), (), s32[]{:S(2)}) async-start(), calls=%async_computation.1 | async-start | bytes 6635520 | tf_op jit(solution)/shard_map/all_gather | solution.py:262
  736.4 56.5 %copy-start.68 = (f32[512]{0:T(512)S(1)}, f32[512]{0:T(512)}, u32[]{:S(2)}) copy-start(f32[512]{0:T(512)} %copy-done.67) | copy-start | bytes 6148
  744.1 52.8 %copy-start.13 = (f32[192,3352]{0,1:T(8,128)S(1)}, f32[192,3352]{0,1:T(8,128)}, u32[]{:S(2)}) copy-start(f32[192,3352]{0,1:T(8,128)} %get-tuple-element.454) | copy-start | bytes 7723012
  (74 other events, 324.3 us)
Sparse Core Ops, SparseCore 0:
  58.8 36.3 all-gather.10
  169.0 70.9 all-gather.12
  359.2 256.4 reduce-scatter.3
  621.6 91.3 all-reduce.16
  717.7 52.3 all-gather.8
  771.5 98.0 all-gather.6
